TPU v7x, 512 devices: a whole 4x4x16 slice. The times are simulated.
512 devices in a mesh: ctx: 64 (over z, x_lo, core), head: 8 (over x_hi, y).
Axes of the slice: x: 4 (x_hi: 2, x_lo: 2; x = x_hi * 2 + x_lo), y: 4, z: 16, core: 2. Of those that a mesh axis runs over, the one named last changes fastest.
Arguments:
- queries: bfloat16 [8192, 6144], P('ctx', 'head'), as said below
- keys: bfloat16 [16384, 1024], P('ctx', 'head'), as said below
- values: bfloat16 [16384, 1024], P('ctx', 'head'), may hold values from -6 to 6
- ranges: int32 [4, 2, 2], replicated, may hold values from 0 to 128, as said below
- noise_ids: int32 [4], replicated, may hold values from 0 to 7
- block_position: int32 [128], replicated, may hold values from 0 to 127, as said below
- level_gain: float32 [8, 6144], P(None, 'head'), may hold values from 0.1 to 1.9
Outputs:
- attended: bfloat16 [8192, 6144], P('ctx', 'head')
Inputs may be any that keep to these rules, and one draw needn't show every extreme that they name: block_position is a permutation of 0 to 127. Each range has start < end and spans 1 to 64 blocks; some range spans exactly 64; ranges of a stretch may intersect. `queries`: entries of order one in most rows; a draw may hold a few rows whose entries are up to about 28 times larger. `keys`: entries of order one.
All inputs are finite; a program needn't handle non-finite values.
Results may differ from a plain program's by a relative error of at most 0.0075.
Values may be sent and summed in bfloat16 or wider, within the bound.
A program may use at most 64 MiB of HBM per device.

v0:
```python
import jax
import jax.numpy as jnp
from jax import lax
from jax.sharding import PartitionSpec as P

D = 6144
HD = 128
BLK = 128
STRETCHES = 4
LEVELS = 8


negative = -1e30


def update(running, query_heads, key_rows, value_rows, live_keys, score_scale):
    top_old, total_old, summed_old = running
    score = (
        jnp.einsum("hrd,nhd->hrn", query_heads, key_rows, preferred_element_type=jnp.float32)
        * score_scale
    )
    score = jnp.where(live_keys[None, None, :], score, negative)
    top_new = jnp.maximum(top_old, jnp.max(score, axis=2))
    correct = jnp.exp(top_old - top_new)
    weight = jnp.exp(score - top_new[:, :, None])
    total_new = total_old * correct + jnp.sum(weight, axis=2)
    weight_bf = weight.astype(jnp.bfloat16)
    summed_new = summed_old * correct[:, :, None] + jnp.einsum(
        "hrn,nhd->hrd", weight_bf, value_rows, preferred_element_type=jnp.float32
    )
    return (top_new, total_new, summed_new)


def body(queries, keys, values, ranges, noise_ids, block_position, level_gain):
    q_rows = queries.shape[0]
    heads_here = keys.shape[1] // HD
    group_size = queries.shape[1] // keys.shape[1]
    score_scale = 1.0 / HD**0.5
    stretch_rows = q_rows * lax.axis_size("ctx") // STRETCHES
    stretch = lax.axis_index("ctx") * q_rows // stretch_rows
    stretch_ranges = lax.dynamic_index_in_dim(ranges, stretch, 0, keepdims=False)
    range_starts = stretch_ranges[:, 0]
    range_ends = stretch_ranges[:, 1]
    query_heads = (
        queries.reshape(q_rows, heads_here, group_size, HD)
        .transpose(1, 0, 2, 3)
        .reshape(heads_here, q_rows * group_size, HD)
    )
    width_rows = q_rows * group_size

    def step_block(running, key_rows, value_rows, live_keys):
        return update(running, query_heads, key_rows, value_rows, live_keys, score_scale)

    initial = (
        jnp.full((heads_here, width_rows), negative, jnp.float32),
        jnp.zeros((heads_here, width_rows), jnp.float32),
        jnp.zeros((heads_here, width_rows, HD), jnp.float32),
    )
    key_piece = lax.all_gather(keys, "ctx", axis=0, tiled=True)
    value_piece = lax.all_gather(values, "ctx", axis=0, tiled=True)
    piece_rows = key_piece.shape[0]
    key_rows = key_piece.reshape(piece_rows, heads_here, HD)
    value_rows = value_piece.reshape(piece_rows, heads_here, HD)
    logical = jnp.take(block_position, jnp.arange(piece_rows, dtype=jnp.int32) // BLK)
    live_keys = jnp.any(
        (logical[None, :] >= range_starts[:, None]) & (logical[None, :] < range_ends[:, None]),
        axis=0,
    )

    def inner(index, held):
        offset = index * 512
        return step_block(
            held,
            lax.dynamic_slice_in_dim(key_rows, offset, 512, 0),
            lax.dynamic_slice_in_dim(value_rows, offset, 512, 0),
            lax.dynamic_slice_in_dim(live_keys, offset, 512, 0),
        )

    top_all, total_all, summed_all = lax.fori_loop(0, piece_rows // 512, inner, initial)
    heads = summed_all / total_all[:, :, None]
    heads = (
        heads.reshape(heads_here, q_rows, group_size, HD)
        .transpose(1, 0, 2, 3)
        .reshape(q_rows, heads_here * group_size * HD)
    )
    square_local = jnp.sum(heads * heads, axis=1)
    square = lax.psum(square_local, "head")
    level = jnp.take(noise_ids, stretch)
    one_hot = (jnp.arange(LEVELS, dtype=jnp.int32) == level).astype(jnp.float32)
    gain_row = jnp.dot(one_hot, level_gain, precision=lax.Precision.HIGHEST)
    return (heads / jnp.sqrt(square / D + 1e-06)[:, None] * gain_row[None, :]).astype(jnp.bfloat16)


def solution(mesh):
    placed = (P("ctx", "head"), P("ctx", "head"), P("ctx", "head"), P(), P(), P(), P(None, "head"))
    return jax.shard_map(
        body, mesh=mesh, in_specs=placed, out_specs=P("ctx", "head"), check_vma=False
    )
```

profile of v0, /device:TPU:1, one launch (start us, length us, event | category | flops | bytes accessed | tf_op | source)
XLA Modules:
  0.0 391.0 jit_solution(5223582062787606065)
XLA Ops:
  10.5 97.2 %gather_fusion = s32[16384]{0:T(1024)S(1)} fusion(s32[128]{0:T(128)S(1)} %copy-done.1, s32[16384]{0:T(1024)S(1)} %broadcast_clamp_fusion), kind=kCustom, calls=%fused_computation | custom fusion | bytes 196608 | tf_op jit(solution)/shard_map/jit(_take)/gather | solution.py:64
  109.3 29.7 %all-gather.3.cloned.1.call-done = bf16[16384,128]{1,0:T(8,128)(2,1)} async-done(((bf16[256,128]{1,0:T(8,128)(2,1)}), bf16[16384,128]{1,0:T(8,128)(2,1)}) %all-gather.3.cloned.1.call-update) | async-done | bytes 4194320 | tf_op jit(solution)/shard_map/all_gather | solution.py:59
  139.0 122.4 %all-gather.5.cloned.1.call-done = bf16[16384,128]{1,0:T(8,128)(2,1)} async-done(((bf16[256,128]{1,0:T(8,128)(2,1)}), bf16[16384,128]{1,0:T(8,128)(2,1)}) %all-gather.5.cloned.1.call-update) | async-done | bytes 4194320 | tf_op jit(solution)/shard_map/all_gather | solution.py:60
  261.3 101.3 %while.19 = (s32[]{:T(128)}, f32[1,768]{1,0:T(1,128)S(1)}, f32[1,768]{1,0:T(1,128)S(1)}, f32[1,768,128]{2,1,0:T(8,128)S(1)}, pred[16384]{0:T(1024)(128)(4,1)S(1)...) while((s32[]{:T(128)}, f32[1,768]{1,0:T(1,128)S(1)}, ...), condition=%wide.region_4.5_spmd.clone, body=%wide.region_1.4_spmd.clone.sunk | while | flops 204378624 | bytes 6017731 | solution.py:79
  263.0 1.4 fusion.41
  264.6 1.3 fusion.37
  266.2 1.4 fusion.41
  267.7 1.3 fusion.37
  269.4 1.4 fusion.41
  270.9 1.3 fusion.37
  272.5 1.4 fusion.41
  274.1 1.3 fusion.37
  275.7 1.4 fusion.41
  277.2 1.3 fusion.37
  278.8 1.4 fusion.41
  280.4 1.3 fusion.37
  282.0 1.4 fusion.41
  283.6 1.3 fusion.37
  285.2 1.4 fusion.41
  286.7 1.3 fusion.37
  288.3 1.4 fusion.41
  289.9 1.3 fusion.37
  291.5 1.4 fusion.41
  294.7 1.4 fusion.41
  297.8 1.4 fusion.41
  301.0 1.4 fusion.41
  304.2 1.4 fusion.41
  307.3 1.4 fusion.41
  310.5 1.4 fusion.41
  313.7 1.4 fusion.41
  316.8 1.4 fusion.41
  320.0 1.4 fusion.41
  321.6 1.3 fusion.37
  323.2 1.4 fusion.41
  326.3 1.4 fusion.41
  329.5 1.4 fusion.41
  332.7 1.4 fusion.41
  335.8 1.4 fusion.41
  337.4 1.3 fusion.37
  339.0 1.4 fusion.41
  342.2 1.4 fusion.41
  345.3 1.4 fusion.41
  348.5 1.4 fusion.41
  351.7 1.4 fusion.41
  354.8 1.4 fusion.41
  358.0 1.4 fusion.41
  361.2 1.4 fusion.41
  363.3 20.1 %psum.7 = f32[128]{0:T(128)S(1)} all-reduce(f32[128]{0:T(128)S(1)} %reduce_sum.31), channel_id=1, replica_groups=mesh['ctx'=64,'head'=8] {'head'}, use_global_device_ids=true, to_apply=%region_7.8 | all-reduce | flops 128 | bytes 1024 | tf_op jit(solution)/shard_map/psum | solution.py:87
  (210 shorter events, 45.5 us)
Async XLA Ops:
  6.5 102.3 %copy-start = (f32[8,768]{1,0:T(8,128)S(1)}, f32[8,768]{1,0:T(8,128)}, u32[]{:S(2)}) copy-start(f32[8,768]{1,0:T(8,128)} %param.15) | copy-start | bytes 73732
  6.5 4.0 %copy-start.1 = (s32[128]{0:T(128)S(1)}, s32[128]{0:T(128)}, u32[]{:S(2)}) copy-start(s32[128]{0:T(128)} %param.14) | copy-start | bytes 1540
  6.5 132.4 %all-gather.3.cloned.1.call-start = ((), (), s32[]{:S(2)}) async-start(), calls=%async_computation | async-start | bytes 4259840 | tf_op jit(solution)/shard_map/all_gather | solution.py:59
  7.3 254.1 %all-gather.5.cloned.1.call-start = ((), (), s32[]{:S(2)}) async-start(), calls=%async_computation.1 | async-start | bytes 4259840 | tf_op jit(solution)/shard_map/all_gather | solution.py:60
  10.5 97.9 %copy-start.2 = (s32[4,2,2]{0,2,1:T(2,128)S(1)}, s32[4,2,2]{0,2,1:T(2,128)}, u32[]{:S(2)}) copy-start(s32[4,2,2]{0,2,1:T(2,128)} %param.12) | copy-start | bytes 196
Sparse Core Ops, SparseCore 0:
  9.5 129.4 all-gather.2
  141.1 120.1 all-gather.4
where the time goes:
time: 395 us; the launch traced here: 391 us
  waiting for transfers between devices  153 us (39%)
  local copies, waits for them, and re-layouts  103 us (26%)
  matrix products  87.4 us (22%)
  blocking collectives  20.1 us (5%)
  between operations  14.2 us (4%)
  other arithmetic  11.3 us (3%)
    all_gather x1, waiting for transfers between devices, body(): value_piece = lax.all_gather(values, 'ctx', axis=0, tiled=True)  122 us
    gather x1, local copies, waits for them, and re-layouts, body(): jnp.take(block_position, jnp.arange(piece_rows, dtype=jnp.int32) // BLK)  97.2 us
    dot_general x32, matrix products, update(): jnp.einsum('hrn,nhd->hrd', weight_bf, value_rows, preferred_element_type=...  46.1 us
    dot_general x32, matrix products, update(): jnp.einsum('hrd,nhd->hrn', query_heads, key_rows, preferred_element_type=...  41.2 us
    all_gather x1, waiting for transfers between devices, body(): key_piece = lax.all_gather(keys, 'ctx', axis=0, tiled=True)  29.7 us
    psum x1, blocking collectives, body(): square = lax.psum(square_local, 'head')  20.1 us
    reduce_sum x32, other arithmetic, update(): total_new = total_old * correct + jnp.sum(weight, axis=2)  8.2 us
  transfers between devices with their start and end apart: 2, of which 2 were waited for; matrix products, arithmetic and copies ran while one was open for 26% of the time, Pallas kernels for 0%

commit v1 on v0

v1 whole, which is shorter than its diff:
```python
import functools

import jax
import jax.numpy as jnp
from jax import lax
from jax.experimental import pallas as pl
from jax.experimental.pallas import tpu as pltpu
from jax.sharding import PartitionSpec as P

D = 6144
HD = 128
BLK = 128
STRETCHES = 4
HEADS = 6
ROWS = 128
OWN = 256
MESH = pl.DeviceIdType.MESH
NEG = -1e30
BIG = 3e38
UNIT = 1.4426950408889634 / HD**0.5


def kernel(
    n_ctx, n_head,
    ranges_ref, noise_ref, pos_ref, q_hbm, k_hbm, v_hbm, gain_ref, out_ref,
    kbuf, vbuf, qall, acc, top, heads, part_out, part_in, lse_out, lse_in, sq_out, sq_in, caps,
    local_sem, ring_send, ring_recv, side_send, side_recv, q_send, q_recv,
    part_send, part_recv, sq_send, sq_recv,
):
    zs = n_ctx // 4
    last = zs // 2
    me = lax.axis_index("ctx")
    head = lax.axis_index("head")
    z = me // 4
    plane = (me // 2) % 2
    core = me % 2
    up = (lax.rem(me + 4, n_ctx), head)
    down = (lax.rem(me + n_ctx - 4, n_ctx), head)
    side = (me + 1 - 2 * core, head)
    twin = (me + 2 - 4 * plane, head)
    peers = [(me, lax.rem(head + j, n_head)) for j in range(1, n_head)]

    barrier = pltpu.get_barrier_semaphore()
    for other in (up, down, side, twin, *peers):
        pl.semaphore_signal(barrier, inc=1, device_id=other, device_id_type=MESH)

    locals_ = [
        pltpu.make_async_copy(k_hbm, kbuf.at[pl.ds(0, OWN)], local_sem.at[0]),
        pltpu.make_async_copy(v_hbm, vbuf.at[pl.ds(0, OWN)], local_sem.at[1]),
    ] + [
        pltpu.make_async_copy(q_hbm.at[:, pl.ds(h * HD, HD)], qall.at[h], local_sem.at[2 + h])
        for h in range(HEADS)
    ]
    for c in locals_:
        c.start()

    def base(d):
        return 512 + (d - 1) * 1024

    def spot(d, way):
        if isinstance(d, int):
            return base(d) + (way * OWN if d < last else 0)
        return base(d) + jnp.where(d < last, way * OWN, 0)

    def shift(d):
        if isinstance(d, int):
            return 512 if d < last else OWN
        return jnp.where(d < last, 512, OWN)

    def rows(start, g):
        start = start + (g % 2) * 128
        if not isinstance(start, int):
            start = pl.multiple_of(start, 128)
        return pl.ds(start, 128)

    def ring(d, way, g):
        buf, hbm = (kbuf, k_hbm) if g < 2 else (vbuf, v_hbm)
        own = isinstance(d, int) and d == 0
        src = hbm.at[pl.ds((g % 2) * 128, 128)] if own else buf.at[rows(spot(d, way), g)]
        return pltpu.make_async_remote_copy(
            src_ref=src,
            dst_ref=buf.at[rows(spot(d + 1, way), g)],
            send_sem=ring_send.at[d, way, g],
            recv_sem=ring_recv.at[d, way, g],
            device_id=(up, down)[way],
            device_id_type=MESH,
        )

    def across(d, way, g):
        buf = kbuf if g < 2 else vbuf
        start = spot(d, way)
        return pltpu.make_async_remote_copy(
            src_ref=buf.at[rows(start, g)],
            dst_ref=buf.at[rows(start + shift(d), g)],
            send_sem=side_send.at[d, way, g],
            recv_sem=side_recv.at[d, way, g],
            device_id=side,
            device_id_type=MESH,
        )

    def across_own(g):
        buf, hbm = ((kbuf, k_hbm), (vbuf, v_hbm))[g]
        return pltpu.make_async_remote_copy(
            src_ref=hbm,
            dst_ref=buf.at[pl.ds(OWN, OWN)],
            send_sem=side_send.at[0, 0, g],
            recv_sem=side_recv.at[0, 0, g],
            device_id=side,
            device_id_type=MESH,
        )

    def query(h):
        return pltpu.make_async_remote_copy(
            src_ref=q_hbm.at[:, pl.ds(h * HD, HD)],
            dst_ref=qall.at[HEADS + h],
            send_sem=q_send.at[h],
            recv_sem=q_recv.at[h],
            device_id=twin,
            device_id_type=MESH,
        )

    def partial(h):
        src, dst = (part_out.at[h], part_in.at[h]) if h < HEADS else (lse_out, lse_in)
        return pltpu.make_async_remote_copy(
            src_ref=src,
            dst_ref=dst,
            send_sem=part_send.at[h],
            recv_sem=part_recv.at[h],
            device_id=twin,
            device_id_type=MESH,
        )

    def square(j):
        return pltpu.make_async_remote_copy(
            src_ref=sq_out,
            dst_ref=sq_in.at[j],
            send_sem=sq_send.at[j],
            recv_sem=sq_recv.at[j],
            device_id=peers[j],
            device_id_type=MESH,
        )

    pl.semaphore_wait(barrier, 4 + n_head - 1)
    for g in range(4):
        for way in (0, 1):
            ring(0, way, g).start()
        if g < 2:
            across_own(g).start()
    for h in range(HEADS):
        query(h).start()

    stretch = me * STRETCHES // n_ctx
    lo0, hi0 = ranges_ref[stretch, 0, 0], ranges_ref[stretch, 0, 1]
    lo1, hi1 = ranges_ref[stretch, 1, 0], ranges_ref[stretch, 1, 1]

    def cap(b, carry):
        far = b - 4
        d = jnp.where(b < 4, 0, far // 8 + 1)
        r = jnp.where(b < 4, b, far % 8)
        short = jnp.logical_or(b < 4, d == last)
        other = jnp.where(short, r // 2, r // 4)
        way = jnp.where(short, 0, (r // 2) % 2)
        from_z = lax.rem(z + zs + jnp.where(way == 0, -d, d), zs)
        device = from_z * 4 + plane * 2 + lax.rem(core + other, 2)
        at = pos_ref[device * 2 + b % 2]
        live = ((at >= lo0) & (at < hi0)) | ((at >= lo1) & (at < hi1))
        caps[b] = jnp.where(live, BIG, NEG).astype(jnp.float32)
        return carry

    lax.fori_loop(0, zs * 4, cap, 0)

    def scores(t, start, n):
        return lax.dot_general(
            qall[t], kbuf[pl.ds(start, n), :], (((1,), (1,)), ((), ())),
            preferred_element_type=jnp.float32,
        )

    def weigh(t, s, limits, first):
        xs = [
            jnp.minimum(s[:, 128 * j : 128 * j + 128], c) for j, c in enumerate(limits)
        ]
        tree = xs
        while len(tree) > 1:
            tree = [
                jnp.maximum(*tree[i : i + 2]) if i + 1 < len(tree) else tree[i]
                for i in range(0, len(tree), 2)
            ]
        new = jnp.broadcast_to(jnp.max(tree[0], axis=1, keepdims=True), (ROWS, 128))
        if first:
            fade = None
        else:
            old = top[t]
            new = jnp.maximum(old, new)
            fade = jnp.exp2((old - new) * UNIT)
        top[t] = new
        ps = [jnp.exp2((x - new) * UNIT).astype(jnp.bfloat16) for x in xs]
        return jnp.concatenate(ps, axis=1), fade

    def gather(t, p, fade, start, n):
        ones = jnp.ones((n, 128), jnp.bfloat16)
        v = jnp.concatenate([vbuf[pl.ds(start, n), :], ones], axis=1)
        o = jnp.dot(p, v, preferred_element_type=jnp.float32)
        if fade is None:
            acc[t] = o
        else:
            a = acc[t]
            acc[t, :, :128] = a[:, :128] * fade + o[:, :128]
            acc[t, :, 128:] = a[:, 128:] * fade + o[:, 128:]

    def attend(tiles, start, n, before=lambda i: None, after=lambda i: None, first=False):
        at = start // 128
        limits = [caps[at + j] for j in range(n // 128)]
        s, p = {}, {}
        for i in range(len(tiles) + 1):
            if i == 0:
                before(0)
                s[0] = scores(tiles[0], start, n)
            if i + 1 < len(tiles):
                before(i + 1)
                s[i + 1] = scores(tiles[i + 1], start, n)
            if i < len(tiles):
                p[i] = weigh(tiles[i], s.pop(i), limits, first)
            if i >= 1:
                gather(tiles[i - 1], *p.pop(i - 1), start, n)
                after(i - 1)

    def step(d, g):
        for way in (0, 1):
            half = (way == 0) == (g < 2)

            def take(way=way):
                ring(d - 1, way, g).wait_recv()

            def on(way=way):
                ring(d, way, g).start()

            def over(way=way):
                across(d, way, g).start()

            if isinstance(d, int):
                if half or d < last:
                    take()
                    if d < (last if half else last - 1):
                        on()
                    over()
            elif half:
                take()
                pl.when(d < last)(on)
                over()
            else:

                @pl.when(d < last)
                def _():
                    take()
                    pl.when(d < last - 1)(on)
                    over()

    def settle(d):
        for g in range(4):
            for way in (0, 1):
                if isinstance(d, int) and d == last and (way == 0) != (g < 2):
                    continue
                across(d, way, g).wait_recv()

    own_tiles = list(range(HEADS))
    twin_tiles = list(range(HEADS, 2 * HEADS))
    for c in locals_:
        c.wait()
    for g in (0, 1):
        across_own(g).wait_recv()
    attend(own_tiles, 0, 512, first=True)
    for g in range(4):
        step(1, g)
    attend(twin_tiles, 0, 512, before=lambda i: query(i).wait_recv(), first=True)

    def turn(d, carry):
        settle(d - 1)

        def before(i):
            if i % 3 == 0:
                step(d, i // 3)

        attend(
            own_tiles + twin_tiles, pl.multiple_of(base(d - 1), 128), 1024, before=before
        )
        return carry

    lax.fori_loop(2, last + 1, turn, 0)

    settle(last)
    lane = lax.broadcasted_iota(jnp.int32, (ROWS, 128), 1)
    lse = [jnp.zeros((ROWS, 128), jnp.float32)]

    def finish(i):
        if i >= HEADS:
            return
        t = twin_tiles[i]
        total = acc[t, :, 128:]
        part_out[i] = (acc[t, :, :128] / total).astype(jnp.bfloat16)
        lse[0] = jnp.where(lane == i, top[t] * UNIT + jnp.log2(total), lse[0])
        if i == HEADS - 1:
            lse_out[...] = lse[0].T[0:8, :]

    def send(i):
        finish(i)
        if 1 <= i <= HEADS + 1:
            partial(i - 1).start()

    attend(twin_tiles + own_tiles, base(last), 512, after=send)

    square_here = jnp.zeros((ROWS, 128), jnp.float32)
    partial(HEADS).wait_recv()
    lse_cols = jnp.concatenate([lse_in[...], jnp.zeros((120, 128), jnp.float32)], axis=0).T
    for h in range(HEADS):
        partial(h).wait_recv()
        there = jnp.broadcast_to(lse_cols[:, h : h + 1], (ROWS, 128))
        here = top[h] * UNIT
        high = jnp.maximum(here, there)
        a, b = jnp.exp2(here - high), jnp.exp2(there - high)
        both = acc[h, :, 128:] * a + b
        value = (acc[h, :, :128] * a + part_in[h].astype(jnp.float32) * b) / both
        heads[h] = value
        square_here = square_here + value * value
    square_here = jnp.broadcast_to(
        jnp.sum(square_here, axis=1, keepdims=True), (ROWS, 128)
    ).T[0:8, :]
    sq_out[...] = square_here

    for g in range(4):
        for way in (0, 1):
            ring(0, way, g).wait_send()
        if g < 2:
            across_own(g).wait_send()
    for j in range(n_head - 1):
        square(j).start()
    for h in range(HEADS):
        query(h).wait_send()
    for h in range(HEADS + 1):
        partial(h).wait_send()

    def sent(d, carry):
        for g in range(4):
            for way in (0, 1):
                across(d, way, g).wait_send()

                @pl.when(jnp.logical_or(d < last - 1, (way == 0) == (g < 2)))
                def _():
                    ring(d, way, g).wait_send()

        return carry

    lax.fori_loop(1, last, sent, 0)
    for g in range(4):
        across(last, 0 if g < 2 else 1, g).wait_send()

    level = noise_ref[stretch]
    gain = gain_ref[pl.ds(level, 1), :]
    square_all = square_here
    for j in range(n_head - 1):
        square(j).wait_recv()
        square_all = square_all + sq_in[j]
    scale = 1.0 / jnp.sqrt(square_all / (HEADS * HD * n_head) + 1e-06)
    scale = jnp.broadcast_to(scale[0:1, :], (128, 128)).T
    for h in range(HEADS):
        out_ref[:, h * HD : (h + 1) * HD] = (
            heads[h] * scale * gain[:, h * HD : (h + 1) * HD]
        ).astype(out_ref.dtype)
    for j in range(n_head - 1):
        square(j).wait_send()


def body(n_ctx, n_head, queries, keys, values, ranges, noise_ids, block_position, level_gain):
    last = n_ctx // 8
    smem = pl.BlockSpec(memory_space=pltpu.SMEM)
    vmem = pl.BlockSpec(memory_space=pltpu.VMEM)
    anywhere = pl.BlockSpec(memory_space=pl.ANY)
    dma = pltpu.SemaphoreType.DMA
    return pl.pallas_call(
        functools.partial(kernel, n_ctx, n_head),
        out_shape=jax.ShapeDtypeStruct((ROWS, HEADS * HD), jnp.bfloat16),
        in_specs=[smem, smem, smem, anywhere, anywhere, anywhere, vmem],
        out_specs=vmem,
        scratch_shapes=[
            pltpu.VMEM((last * 1024, HD), jnp.bfloat16),
            pltpu.VMEM((last * 1024, HD), jnp.bfloat16),
            pltpu.VMEM((2 * HEADS, ROWS, HD), jnp.bfloat16),
            pltpu.VMEM((2 * HEADS, ROWS, 256), jnp.float32),
            pltpu.VMEM((2 * HEADS, ROWS, 128), jnp.float32),
            pltpu.VMEM((HEADS, ROWS, HD), jnp.float32),
            pltpu.VMEM((HEADS, ROWS, HD), jnp.bfloat16),
            pltpu.VMEM((HEADS, ROWS, HD), jnp.bfloat16),
            pltpu.VMEM((8, 128), jnp.float32),
            pltpu.VMEM((8, 128), jnp.float32),
            pltpu.VMEM((8, 128), jnp.float32),
            pltpu.VMEM((n_head - 1, 8, 128), jnp.float32),
            pltpu.SMEM((last * 8,), jnp.float32),
            dma((2 + HEADS,)),
            dma((last, 2, 4)),
            dma((last, 2, 4)),
            dma((last + 1, 2, 4)),
            dma((last + 1, 2, 4)),
            dma((HEADS,)),
            dma((HEADS,)),
            dma((HEADS + 1,)),
            dma((HEADS + 1,)),
            dma((n_head - 1,)),
            dma((n_head - 1,)),
        ],
        compiler_params=pltpu.CompilerParams(
            collective_id=0, has_side_effects=True, vmem_limit_bytes=48 << 20
        ),
        name="attend",
    )(ranges, noise_ids, block_position, queries, keys, values, level_gain)


def solution(mesh):
    placed = (P("ctx", "head"), P("ctx", "head"), P("ctx", "head"), P(), P(), P(), P(None, "head"))
    return jax.shard_map(
        functools.partial(body, mesh.shape["ctx"], mesh.shape["head"]),
        mesh=mesh, in_specs=placed, out_specs=P("ctx", "head"), check_vma=False,
    )
```

time: 395 us -> 66.2 us (0.17)
  waiting for transfers between devices: 153 us -> 0 us
  local copies, waits for them, and re-layouts: 103 us -> 4.83 us
  matrix products: 87.4 us -> 0 us
  Pallas kernels: 0 us -> 61 us
  blocking collectives: 20.1 us -> 0 us
  between operations: 14.2 us -> 0.02 us
  other arithmetic: 11.3 us -> 0 us
    all_gather x2 -> x0, waiting for transfers between devices: 152 us -> none  [the longest x1 122 us: body(): value_piece = lax.all_gather(values, 'ctx', axis=0, tiled=True)]
    gather x1 -> x0, local copies, waits for them, and re-layouts: 97.2 us -> none  [body(): jnp.take(block_position, jnp.arange(piece_rows, dtype=jnp.int32) // BLK)]
    dot_general x65 -> x0, matrix products: 87.4 us -> none  [the longest x32 46.1 us: update(): jnp.einsum('hrn,nhd->hrd', weight_bf, value_rows, preferred_element_type=...]
    pallas_call x0 -> x1, Pallas kernels: none -> 61 us  [body(): pl.pallas_call(functools.partial(kernel, n_ctx, n_head), out_shape=jax.Sh...]
    psum x1 -> x0, blocking collectives: 20.1 us -> none  [body(): square = lax.psum(square_local, 'head')]
    reduce_sum x34 -> x0, other arithmetic: 8.6 us -> none  [the longest x32 8.2 us: update(): total_new = total_old * correct + jnp.sum(weight, axis=2)]
    unnamed x6 -> x14, local copies, waits for them, and re-layouts: 0.01 us -> 4.83 us
  transfers between devices with their start and end apart: 2 -> 0, of which waited for: 2 -> 0; matrix products, arithmetic and copies ran while one was open for 26% -> 0% of each run, Pallas kernels for 0% -> 0%
where the time goes in v1:
time: 66.2 us; the launch traced here: 65.8 us
  Pallas kernels  61 us (92%)
  local copies, waits for them, and re-layouts  4.83 us (7%)
    pallas_call x1, Pallas kernels, body(): pl.pallas_call(functools.partial(kernel, n_ctx, n_head), out_shape=jax.Sh...  61 us
    unnamed x14, local copies, waits for them, and re-layouts  4.83 us

profile of v1, /device:TPU:1, one launch (start us, length us, event | category | flops | bytes accessed | tf_op | source)
XLA Modules:
  0.0 65.8 jit_solution(1275315458849733742)
XLA Ops:
  0.0 0.0 copy-start.5
  0.0 0.0 copy-start.4
  0.0 0.8 %copy.8.ranges_ref = s32[4,2,2]{2,1,0:T(2,128)S(1)} copy(s32[4,2,2]{0,2,1:T(2,128)} %param.10) | data formatting | bytes 128 | tf_op args[3]
  0.8 0.0 copy-done.5
  0.8 0.0 copy-done.4
  0.8 0.0 copy-start
  0.8 0.9 %copy-done = bf16[128,768]{1,0:T(8,128)(2,1)S(1)} copy-done((bf16[128,768]{1,0:T(8,128)(2,1)S(1)}, bf16[128,768]{1,0:T(8,128)(2,1)}, u32[]{:S(2)}) %copy-start) | copy-done | bytes 196632
  1.7 0.0 copy-start.1
  1.7 0.8 %copy-done.1 = bf16[256,128]{1,0:T(8,128)(2,1)S(1)} copy-done((bf16[256,128]{1,0:T(8,128)(2,1)S(1)}, bf16[256,128]{1,0:T(8,128)(2,1)}, u32[]{:S(2)}) %copy-start.1) | copy-done | bytes 65560
  2.6 0.0 copy-start.2
  2.6 0.8 %copy-done.2 = bf16[256,128]{1,0:T(8,128)(2,1)S(1)} copy-done((bf16[256,128]{1,0:T(8,128)(2,1)S(1)}, bf16[256,128]{1,0:T(8,128)(2,1)}, u32[]{:S(2)}) %copy-start.2) | copy-done | bytes 65560
  3.4 0.0 copy-start.3
  3.4 0.7 %copy-done.3 = f32[8,768]{1,0:T(8,128)S(1)} copy-done((f32[8,768]{1,0:T(8,128)S(1)}, f32[8,768]{1,0:T(8,128)}, u32[]{:S(2)}) %copy-start.3) | copy-done | bytes 24600
  4.2 61.0 %attend.1 = bf16[128,768]{1,0:T(8,128)(2,1)S(1)} custom-call(s32[4,2,2]{2,1,0:T(2,128)S(1)} %copy.8.ranges_ref, s32[4]{0:T(128)S(1)} %copy-done.4, s32[128]{0:T(128)S(1)} %copy-done.5, bf16[128,768]{1,0:T(8,128)(2,1)S(1)} %copy-done, bf16[256,128]{1,0:T(8,128)(2,1)S(1)} %copy-done.1, bf16[256,128]{1,0:T(8,128)(2,1)S(1)} %copy-done.2, f32[8,768]{1,0:T(8,128)S(1)} %copy-done.3), custom_call_target="tpu_custom_call" | custom-call | tf_op jit(solution)/shard_map/attend/pallas_call | solution.py:378
  65.2 0.7 %copy.10 = bf16[128,768]{1,0:T(8,128)(2,1)} copy(bf16[128,768]{1,0:T(8,128)(2,1)S(1)} %attend.1) | data formatting | bytes 393216
Async XLA Ops:
  0.0 0.8 %copy-start.5 = (s32[128]{0:T(128)S(1)}, s32[128]{0:T(128)}, u32[]{:S(2)}) copy-start(s32[128]{0:T(128)} %pos_ref.1) | copy-start | bytes 1540
  0.0 0.8 %copy-start.4 = (s32[4]{0:T(128)S(1)}, s32[4]{0:T(128)}, u32[]{:S(2)}) copy-start(s32[4]{0:T(128)} %noise_ref.1) | copy-start | bytes 52
  0.8 0.9 %copy-start = (bf16[128,768]{1,0:T(8,128)(2,1)S(1)}, bf16[128,768]{1,0:T(8,128)(2,1)}, u32[]{:S(2)}) copy-start(bf16[128,768]{1,0:T(8,128)(2,1)} %q_hbm.1) | copy-start | bytes 589828
  1.7 0.8 %copy-start.1 = (bf16[256,128]{1,0:T(8,128)(2,1)S(1)}, bf16[256,128]{1,0:T(8,128)(2,1)}, u32[]{:S(2)}) copy-start(bf16[256,128]{1,0:T(8,128)(2,1)} %k_hbm.1) | copy-start | bytes 196612
  2.6 0.8 %copy-start.2 = (bf16[256,128]{1,0:T(8,128)(2,1)S(1)}, bf16[256,128]{1,0:T(8,128)(2,1)}, u32[]{:S(2)}) copy-start(bf16[256,128]{1,0:T(8,128)(2,1)} %v_hbm.1) | copy-start | bytes 196612
  3.4 0.7 %copy-start.3 = (f32[8,768]{1,0:T(8,128)S(1)}, f32[8,768]{1,0:T(8,128)}, u32[]{:S(2)}) copy-start(f32[8,768]{1,0:T(8,128)} %gain_ref.1) | copy-start | bytes 73732
